TPU v7x, 512 devices: a whole 4x8x8 slice. The times are simulated.
512 devices in a mesh: stream: 16 (over z, x_hi), span: 32 (over y, x_lo, core).
Axes of the slice: x: 4 (x_hi: 2, x_lo: 2; x = x_hi * 2 + x_lo), y: 8, z: 8, core: 2. Of those that a mesh axis runs over, the one named last changes fastest.
Arguments:
- pre_pops: float32 [19, 128, 256, 128], P(None, 'stream', 'span'), may hold values from 0.7 to 1.3
- main_pops: float32 [19, 128, 256, 256], P(None, 'stream', 'span'), may hold values from 0.7 to 1.3
- tile_map: int32 [32], replicated, may hold values from 0 to 31, each once
- layer_phase: int32 [32], replicated, may hold values from 0 to 1
- wall_flags: int32 [256], replicated, may hold values 0 or 1
Outputs:
- pre_out: float32 [19, 128, 256, 128], P(None, 'stream', 'span')
- main_out: float32 [19, 128, 256, 256], P(None, 'stream', 'span')
Inputs may be any that keep to these rules, and one draw needn't show every extreme that they name: `tile_map`: each precursor tile feeds exactly one inlet tile.
All inputs are finite; a program needn't handle non-finite values.
Results may differ from a plain program's by a relative error of at most 0.0003.
Values sent between devices are 32-bit elements; how exact they have to be, the bound alone decides.
A program may use at most 64 MiB of HBM per device.

v0:
```python
import jax
import jax.numpy as jnp
from jax import lax
from jax.experimental import pallas as pl
from jax.experimental.pallas import tpu as pltpu

VELOCITIES = (
    (0, 0, 0),
    (1, 0, 0), (-1, 0, 0), (0, 1, 0), (0, -1, 0), (0, 0, 1), (0, 0, -1),
    (1, 1, 0), (-1, -1, 0), (1, -1, 0), (-1, 1, 0),
    (1, 0, 1), (-1, 0, -1), (1, 0, -1), (-1, 0, 1),
    (0, 1, 1), (0, -1, -1), (0, 1, -1), (0, -1, 1),
)
OPPOSITE = (0, 2, 1, 4, 3, 6, 5, 8, 7, 10, 9, 12, 11, 14, 13, 16, 15, 18, 17)
ORDER = (1, 7, 9, 11, 13, 2, 8, 10, 12, 14, 0, 3, 4, 5, 6, 15, 16, 17, 18)
POS = tuple(ORDER.index(i) for i in range(19))
Z_UP = (5, 11, 14, 15, 18)
Z_DOWN = (6, 12, 13, 16, 17)
PAIRS = ((1, 2), (3, 4), (5, 6), (7, 8), (9, 10), (11, 12), (13, 14), (15, 16), (17, 18))
CX, CZ = 8, 8
NP, NM = 128, 256
LANES = NP + NM
STREAM, SPAN = 16, 32
ROWS, COLS = 8, 4
MESH = pl.DeviceIdType.MESH


def collide_planes(load, store, x):
    for lane in range(3):
        g = [load(i, x, lane) for i in range(19)]
        diff = {a: g[a] - g[b] for a, b in PAIRS}
        both = {a: g[a] + g[b] for a, b in PAIRS}
        axes = both[1] + both[3] + both[5]
        edges = (both[7] + both[9]) + (both[11] + both[13]) + (both[15] + both[17])
        density = (1.0 / 3.0) * g[0] + (1.0 / 18.0) * axes + (1.0 / 36.0) * edges
        mx = (1.0 / 18.0) * diff[1] + (1.0 / 36.0) * ((diff[7] + diff[9]) + (diff[11] + diff[13]))
        my = (1.0 / 18.0) * diff[3] + (1.0 / 36.0) * ((diff[7] - diff[9]) + (diff[15] + diff[17]))
        mz = (1.0 / 18.0) * diff[5] + (1.0 / 36.0) * ((diff[11] - diff[13]) + (diff[15] - diff[17]))
        inverse = 1.0 / density
        base = 1.25 * density - (1.875 * inverse) * (mx * mx + my * my + mz * mz)
        scale = 5.625 * inverse
        store(0, x, lane, base - 0.25 * g[0])
        moment = (mx, my, mz)
        for a, b in PAIRS:
            along = None
            for axis in range(3):
                c = VELOCITIES[a][axis]
                if c:
                    term = moment[axis]
                    if along is None:
                        along = term
                    else:
                        along = along + term if c > 0 else along - term
            even = base + scale * (along * along)
            odd = 3.75 * along
            store(a, x, lane, (even + odd) - 0.25 * g[a])
            store(b, x, lane, (even - odd) - 0.25 * g[b])


def body(tile_ref, phase_ref, wall_ref, pre_ref, main_ref, pre_out, main_out,
         star, zsend, zrecv, temp, masks, spread, rows_a, rows_b, pay_send, pay_a, pay_b,
         xs_sem, xr_sem, zs_sem, zr_sem, cs_sem, cr_sem, ys_sem, yr_sem, qs_sem, qr_sem):
    rows_buf, pay_recv = (rows_a, rows_b), (pay_a, pay_b)
    st = lax.axis_index("stream")
    sp = lax.axis_index("span")
    st_up, st_down = lax.rem(st + 1, STREAM), lax.rem(st + STREAM - 1, STREAM)
    sp_up, sp_down = lax.rem(sp + 1, SPAN), lax.rem(sp + SPAN - 1, SPAN)
    row, col = lax.div(sp, COLS), lax.rem(sp, COLS)

    barrier = pltpu.get_barrier_semaphore()
    for a in (st_up, st, st_down):
        for b in (sp_up, sp, sp_down):
            if a is st and b is sp:
                continue
            pl.semaphore_signal(barrier, inc=1, device_id=(a, b), device_id_type=MESH)

    @pl.when(st == 0)
    def _():
        for d in range(1, ROWS):
            peer = lax.rem(row + d, ROWS) * COLS + col
            pl.semaphore_signal(barrier, inc=1, device_id=(st, peer), device_id_type=MESH)
        for e in range(1, COLS):
            peer = row * COLS + lax.rem(col + e, COLS)
            pl.semaphore_signal(barrier, inc=1, device_id=(st, peer), device_id_type=MESH)

    def remote(src, dst, send, recv, device):
        return pltpu.make_async_remote_copy(
            src_ref=src, dst_ref=dst, send_sem=send, recv_sem=recv,
            device_id=device, device_id_type=MESH)

    def x_copy(step, way):
        if way == 0:
            return remote(star.at[step, 0:5, CX], star.at[step, 0:5, 0],
                          xs_sem.at[step, 0], xr_sem.at[step, 0], (st_up, sp))
        return remote(star.at[step, 5:10, 1], star.at[step, 5:10, CX + 1],
                      xs_sem.at[step, 1], xr_sem.at[step, 1], (st_down, sp))

    def z_copy(step, way):
        return remote(zsend.at[step, way], zrecv.at[step, way, :, 1:CX + 1],
                      zs_sem.at[step, way], zr_sem.at[step, way],
                      (st, sp_up if way == 0 else sp_down))

    def corner_copy(step, which):
        way, pop, x, slot, device = (
            (0, Z_UP.index(11), CX - 1, 0, (st_up, sp_up)),
            (0, Z_UP.index(14), 0, CX + 1, (st_down, sp_up)),
            (1, Z_DOWN.index(12), 0, CX + 1, (st_down, sp_down)),
            (1, Z_DOWN.index(13), CX - 1, 0, (st_up, sp_down)),
        )[which]
        return remote(zsend.at[step, way, pop, x], zrecv.at[step, way, pop, slot],
                      cs_sem.at[step, which], cr_sem.at[step, which], device)

    def row_copy(step, d):
        peer = lax.rem(row + d, ROWS) * COLS + col
        return remote(star.at[step, 0:5, CX, :, 0:NP], rows_buf[step].at[d],
                      ys_sem.at[step, d], yr_sem.at[step, d], (st, peer))

    def quad_copy(step, e):
        peer = row * COLS + lax.rem(col + e, COLS)
        return remote(pay_send.at[step, e], pay_recv[step].at[e],
                      qs_sem.at[step, e], qr_sem.at[step, e], (st, peer))

    def lanes(lane):
        return slice(lane * 128, lane * 128 + 128)

    def load_input(i, x, lane):
        if lane == 0:
            return pre_ref[i, x]
        return main_ref[i, x, :, lanes(lane - 1)]

    def load_temp(i, x, lane):
        return temp[i, :, lanes(lane)]

    def store_star(step):
        def store(i, x, lane, value):
            star[step, POS[i], x + 1, :, lanes(lane)] = value
            if i in Z_UP:
                zsend[step, 0, Z_UP.index(i), x, :, lanes(lane)] = value[CZ - 1:CZ, :]
            if i in Z_DOWN:
                zsend[step, 1, Z_DOWN.index(i), x, :, lanes(lane)] = value[0:1, :]
        return store

    row_id = lax.broadcasted_iota(jnp.int32, (CZ, LANES), 0)

    def stream_plane(step, x, write):
        for i in range(19):
            cx, cy, cz = VELOCITIES[i]
            source = star[step, POS[i], x + 1 - cx]
            if cz == 1:
                edge = zrecv[step, 0, Z_UP.index(i), x + 1 - cx]
                source = jnp.where(row_id == 0, jnp.broadcast_to(edge, (CZ, LANES)),
                                   pltpu.roll(source, 1, 0))
            elif cz == -1:
                edge = zrecv[step, 1, Z_DOWN.index(i), x + 1 - cx]
                source = jnp.where(row_id == CZ - 1, jnp.broadcast_to(edge, (CZ, LANES)),
                                   pltpu.roll(source, CZ - 1, 0))
            if cy == 1:
                source = pltpu.roll(source, 1, 1)
            elif cy == -1:
                source = pltpu.roll(source, LANES - 1, 1)
            write(i, jnp.where(masks[cy % 3] > 0.5, star[step, POS[OPPOSITE[i]], x + 1], source))

    def write_temp(i, value):
        temp[i] = value

    def advance(x):
        stream_plane(0, x, write_temp)
        collide_planes(load_temp, store_star(1), x)

    def finish(x):
        def write(i, value):
            pre_out[i, x] = value[:, 0:NP]
            main_out[i, x] = value[:, NP:]
        stream_plane(1, x, write)

    def rows_start(step):
        @pl.when(st == 0)
        def _():
            for d in range(1, ROWS):
                row_copy(step, d).start()
            rows_buf[step][0] = star[step, 0:5, CX, :, 0:NP]

    small_row = lax.broadcasted_iota(jnp.int32, (CZ, 128), 0)

    def row_slot(tile):
        return lax.rem(row - lax.div(tile, COLS) + ROWS, ROWS)

    def col_slot(tile):
        return lax.rem(col - lax.rem(tile, COLS) + COLS, COLS)

    def quads_start(step):
        @pl.when(st == 0)
        def _():
            for d in range(1, ROWS):
                row_copy(step, d).wait()
            for e in range(COLS):
                target = row * COLS + lax.rem(col + e, COLS)
                own = tile_ref[target]
                left = tile_ref[lax.rem(target + SPAN - 1, SPAN)]
                right = tile_ref[lax.rem(target + 1, SPAN)]
                out = pay_recv[step].at[0] if e == 0 else pay_send.at[step, e]
                out[0:5] = rows_buf[step][row_slot(own)]
                out[5] = jnp.where(
                    small_row == 0,
                    pltpu.roll(rows_buf[step][row_slot(left), 3], 1, 0),
                    pltpu.roll(rows_buf[step][row_slot(right), 4], 1, 0))
                if e:
                    quad_copy(step, e).start()

    def inlet(step):
        @pl.when(st == 0)
        def _():
            for e in range(1, COLS):
                quad_copy(step, e).wait()
            left_at = lax.rem(sp + SPAN - 1, SPAN)
            right_at = lax.rem(sp + 1, SPAN)
            tile = pay_recv[step][col_slot(tile_ref[sp]), 0:5]
            edge = jnp.where(small_row == 0,
                             pay_recv[step][col_slot(tile_ref[left_at]), 5],
                             pay_recv[step][col_slot(tile_ref[right_at]), 5])
            coarse = jnp.concatenate([tile.reshape(5 * CZ, 128), edge], axis=0)
            fine = jnp.dot(coarse, spread[...], precision=lax.Precision.HIGHEST,
                           preferred_element_type=jnp.float32)
            own_phase = jnp.full((5 * CZ, NM), phase_ref[sp], jnp.int32)
            plane = jnp.where(own_phase == 0, fine[0:5 * CZ, 0:NM], fine[0:5 * CZ, NM:])
            plane = plane.reshape(5, CZ, NM)
            for k in range(5):
                star[step, k, 0, :, NP:] = plane[k]
            tail = fine[5 * CZ:, :]
            left_phase = jnp.full((CZ, NM), phase_ref[left_at], jnp.int32)
            right_phase = jnp.full((CZ, NM), phase_ref[right_at], jnp.int32)
            left = jnp.where(left_phase == 0, tail[:, 0:NM], tail[:, NM:])
            right = jnp.where(right_phase == 0, tail[:, 0:NM], tail[:, NM:])
            zrecv[step, 0, Z_UP.index(11), 0, :, NP:] = left[0:1]
            zrecv[step, 1, Z_DOWN.index(13), 0, :, NP:] = right[1:2]

    def outlet(step):
        @pl.when(st == STREAM - 1)
        def _():
            for k in range(5, 10):
                star[step, k, CX + 1, :, NP:] = star[step, k, CX, :, NP:]
            for way, pop in ((0, Z_UP.index(14)), (1, Z_DOWN.index(12))):
                zrecv[step, way, pop, CX + 1, :, NP:] = zrecv[step, way, pop, CX, :, NP:]

    collide_planes(load_input, store_star(0), CX - 1)

    @pl.when(st == 0)
    def _():
        pl.semaphore_wait(barrier, 8 + ROWS + COLS - 2)

    @pl.when(st != 0)
    def _():
        pl.semaphore_wait(barrier, 8)

    x_copy(0, 0).start()
    rows_start(0)
    collide_planes(load_input, store_star(0), 0)
    x_copy(0, 1).start()

    def first(x, carry):
        collide_planes(load_input, store_star(0), x)
        return carry

    lax.fori_loop(1, CX - 1, first, 0)
    for way in range(2):
        z_copy(0, way).start()
    for which in range(4):
        corner_copy(0, which).start()

    wall = jnp.broadcast_to(wall_ref[...].astype(jnp.float32), (CZ, NM))
    fine_id = lax.broadcasted_iota(jnp.int32, (NM, NP), 0)
    coarse_id = lax.broadcasted_iota(jnp.int32, (NM, NP), 1)
    pick = jnp.where(lax.shift_right_logical(fine_id, 1) == coarse_id, 1.0, 0.0)
    merged = jnp.dot(wall, pick, preferred_element_type=jnp.float32)
    coarse_wall = jnp.where(merged > 0.5, 1.0, 0.0)
    solid = jnp.concatenate([coarse_wall, wall], axis=1)
    lane_id = lax.broadcasted_iota(jnp.int32, (CZ, LANES), 1)
    masks[0] = solid
    masks[1] = jnp.where((lane_id == 0) | (lane_id == NP), 1.0, pltpu.roll(solid, 1, 1))
    masks[2] = jnp.where((lane_id == NP - 1) | (lane_id == LANES - 1), 1.0,
                         pltpu.roll(solid, LANES - 1, 1))

    @pl.when(st == 0)
    def _():
        coarse_row = lax.broadcasted_iota(jnp.int32, (NP, NM), 0)
        fine_col = lax.broadcasted_iota(jnp.int32, (NP, NM), 1)
        for phase in range(2):
            place = fine_col + phase
            lower = lax.shift_right_arithmetic(place - 1, 1)
            upper = jnp.where((place & 1) == 0, 0.75, 0.25)
            low = jnp.clip(lower, 0, NP - 1)
            high = jnp.clip(lower + 1, 0, NP - 1)
            spread[:, phase * NM:(phase + 1) * NM] = (
                jnp.where(coarse_row == low, 1.0 - upper, 0.0)
                + jnp.where(coarse_row == high, upper, 0.0))

    for step in range(2):
        plane = advance if step == 0 else finish

        def inner(x, carry):
            plane(x)
            return carry

        for way in range(2):
            z_copy(step, way).wait()
        lax.fori_loop(1, CX - 1, inner, 0)
        quads_start(step)
        for way in range(2):
            x_copy(step, way).wait()
        for which in range(4):
            corner_copy(step, which).wait()
        outlet(step)
        plane(CX - 1)
        if step == 0:
            x_copy(1, 0).start()
            rows_start(1)
        inlet(step)
        plane(0)
        if step == 0:
            x_copy(1, 1).start()
            for way in range(2):
                z_copy(1, way).start()
            for which in range(4):
                corner_copy(1, which).start()


def local(pre_pops, main_pops, tile_map, layer_phase, wall_flags):
    vmem = pl.BlockSpec(memory_space=pltpu.VMEM)
    smem = pl.BlockSpec(memory_space=pltpu.SMEM)
    dma = pltpu.SemaphoreType.DMA
    f32 = jnp.float32
    return pl.pallas_call(
        body,
        out_shape=(jax.ShapeDtypeStruct(pre_pops.shape, f32),
                   jax.ShapeDtypeStruct(main_pops.shape, f32)),
        in_specs=[smem, smem, vmem, vmem, vmem],
        out_specs=(vmem, vmem),
        scratch_shapes=[
            pltpu.VMEM((2, 19, CX + 2, CZ, LANES), f32),
            pltpu.VMEM((2, 2, 5, CX, 1, LANES), f32),
            pltpu.VMEM((2, 2, 5, CX + 2, 1, LANES), f32),
            pltpu.VMEM((19, CZ, LANES), f32),
            pltpu.VMEM((3, CZ, LANES), f32),
            pltpu.VMEM((NP, 2 * NM), f32),
            pltpu.VMEM((ROWS, 5, CZ, NP), f32),
            pltpu.VMEM((ROWS, 5, CZ, NP), f32),
            pltpu.VMEM((2, COLS, 6, CZ, NP), f32),
            pltpu.VMEM((COLS, 6, CZ, NP), f32),
            pltpu.VMEM((COLS, 6, CZ, NP), f32),
            dma((2, 2)), dma((2, 2)), dma((2, 2)), dma((2, 2)),
            dma((2, 4)), dma((2, 4)),
            dma((2, ROWS)), dma((2, ROWS)), dma((2, COLS)), dma((2, COLS)),
        ],
        compiler_params=pltpu.CompilerParams(
            collective_id=0, has_side_effects=True, vmem_limit_bytes=60 * 1024 * 1024),
    )(tile_map, layer_phase, wall_flags.reshape(1, NM), pre_pops, main_pops)


def solution(mesh):
    spec = jax.sharding.PartitionSpec
    blocks = spec(None, "stream", "span", None)
    return jax.shard_map(
        local,
        mesh=mesh,
        in_specs=(blocks, blocks, spec(), spec(), spec()),
        out_specs=(blocks, blocks),
        check_vma=False,
    )
```

profile of v0, /device:TPU:1, one launch (start us, length us, event | category | flops | bytes accessed | tf_op | source)
XLA Modules:
  0.0 41.1 jit_solution(3261997158465905359)
XLA Ops:
  0.6 37.3 %shard_map.68 = (f32[19,8,8,128]{3,2,1,0:T(8,128)}, f32[19,8,8,256]{3,2,1,0:T(8,128)}) custom-call(s32[32]{0:T(128)} %tile_ref.1, s32[32]{0:T(128)} %phase_ref.1, s32[1,256]{1,0:T(1,128)} %bitcast.1, f32[19,8,8,128]{3,2,1,0:T(8,128)} %pre_ref.1, f32[19,8,8,256]{3,2,1,0:T(8,128)} %main_ref.1), custom_call_target="tpu_custom_call" | custom-call | tf_op jit(solution)/shard_map/pallas_call | solution.py:332
  38.0 0.0 copy-start
  38.0 2.1 %copy.9 = f32[19,8,8,128]{3,2,1,0:T(8,128)} copy(f32[19,8,8,128]{3,2,1,0:T(8,128)} %get-tuple-element.4) | data formatting | bytes 1245184
  40.0 0.0 copy-done
  40.1 1.0 %copy.10 = f32[19,8,8,256]{3,2,1,0:T(8,128)} copy(f32[19,8,8,256]{3,2,1,0:T(8,128)S(1)} %copy-done) | data formatting | bytes 2490368
Async XLA Ops:
  38.0 2.1 %copy-start = (f32[19,8,8,256]{3,2,1,0:T(8,128)S(1)}, f32[19,8,8,256]{3,2,1,0:T(8,128)}, u32[]{:S(2)}) copy-start(f32[19,8,8,256]{3,2,1,0:T(8,128)} %get-tuple-element.5) | copy-start | bytes 3735556
where the time goes:
time: 41.3 us; the launch traced here: 41.1 us
  Pallas kernels  37.3 us (90%)
  local copies, waits for them, and re-layouts  3.1 us (8%)
  between operations  0.65 us (2%)
    pallas_call x1, Pallas kernels, local(): pl.pallas_call(body, out_shape=(jax.ShapeDtypeStruct(pre_pops.shape, f32)...  37.3 us
    unnamed x4, local copies, waits for them, and re-layouts  3.1 us

commit v1 on v0

--- a/solution.py
+++ b/solution.py
@@ -25,8 +25,8 @@
 MESH = pl.DeviceIdType.MESH
 
 
-def collide_planes(load, store, x):
-    for lane in range(3):
+def collide_planes(load, store, x, chunks=(0, 1, 2)):
+    for lane in chunks:
         g = [load(i, x, lane) for i in range(19)]
         diff = {a: g[a] - g[b] for a, b in PAIRS}
         both = {a: g[a] + g[b] for a, b in PAIRS}
@@ -57,9 +57,9 @@
             store(b, x, lane, (even - odd) - 0.25 * g[b])
 
 
-def body(tile_ref, phase_ref, wall_ref, pre_ref, main_ref, pre_out, main_out,
-         star, zsend, zrecv, temp, masks, spread, rows_a, rows_b, pay_send, pay_a, pay_b,
-         xs_sem, xr_sem, zs_sem, zr_sem, cs_sem, cr_sem, ys_sem, yr_sem, qs_sem, qr_sem):
+def body(tile_hbm, phase_hbm, wall_hbm, pre_hbm, main_hbm, pre_out, main_out,
+         tile_ref, phase_ref, wall_ref, pre_ref, main_ref, star, zsend, zrecv, temp, masks, spread, rows_a, rows_b, pay_send, pay_a, pay_b,
+         xs_sem, xr_sem, zs_sem, zr_sem, cs_sem, cr_sem, ys_sem, yr_sem, qs_sem, qr_sem, in_sem):
     rows_buf, pay_recv = (rows_a, rows_b), (pay_a, pay_b)
     st = lax.axis_index("stream")
     sp = lax.axis_index("span")
@@ -83,17 +83,27 @@
             peer = row * COLS + lax.rem(col + e, COLS)
             pl.semaphore_signal(barrier, inc=1, device_id=(st, peer), device_id_type=MESH)
 
+    loads = [pltpu.make_async_copy(source, target, in_sem.at[at])
+             for at, (source, target) in enumerate((
+                 (pre_hbm, pre_ref), (main_hbm, main_ref), (wall_hbm, wall_ref),
+                 (tile_hbm, tile_ref), (phase_hbm, phase_ref)))]
+    for load in loads:
+        load.start()
+
     def remote(src, dst, send, recv, device):
         return pltpu.make_async_remote_copy(
             src_ref=src, dst_ref=dst, send_sem=send, recv_sem=recv,
             device_id=device, device_id_type=MESH)
 
-    def x_copy(step, way):
+    PRE, MAIN = slice(0, NP), slice(NP, LANES)
+
+    def x_copy(step, way, part):
+        cut = (PRE, MAIN)[part]
         if way == 0:
-            return remote(star.at[step, 0:5, CX], star.at[step, 0:5, 0],
-                          xs_sem.at[step, 0], xr_sem.at[step, 0], (st_up, sp))
-        return remote(star.at[step, 5:10, 1], star.at[step, 5:10, CX + 1],
-                      xs_sem.at[step, 1], xr_sem.at[step, 1], (st_down, sp))
+            return remote(star.at[step, 0:5, CX, :, cut], star.at[step, 0:5, 0, :, cut],
+                          xs_sem.at[step, 0, part], xr_sem.at[step, 0, part], (st_up, sp))
+        return remote(star.at[step, 5:10, 1, :, cut], star.at[step, 5:10, CX + 1, :, cut],
+                      xs_sem.at[step, 1, part], xr_sem.at[step, 1, part], (st_down, sp))
 
     def z_copy(step, way):
         return remote(zsend.at[step, way], zrecv.at[step, way, :, 1:CX + 1],
@@ -140,38 +150,38 @@
                 zsend[step, 1, Z_DOWN.index(i), x, :, lanes(lane)] = value[0:1, :]
         return store
 
-    row_id = lax.broadcasted_iota(jnp.int32, (CZ, LANES), 0)
-
-    def stream_plane(step, x, write):
+    def stream_plane(step, x, cut, write):
+        width = cut.stop - cut.start
+        row_id = lax.broadcasted_iota(jnp.int32, (CZ, width), 0)
         for i in range(19):
             cx, cy, cz = VELOCITIES[i]
-            source = star[step, POS[i], x + 1 - cx]
+            source = star[step, POS[i], x + 1 - cx, :, cut]
             if cz == 1:
-                edge = zrecv[step, 0, Z_UP.index(i), x + 1 - cx]
-                source = jnp.where(row_id == 0, jnp.broadcast_to(edge, (CZ, LANES)),
+                edge = zrecv[step, 0, Z_UP.index(i), x + 1 - cx, :, cut]
+                source = jnp.where(row_id == 0, jnp.broadcast_to(edge, (CZ, width)),
                                    pltpu.roll(source, 1, 0))
             elif cz == -1:
-                edge = zrecv[step, 1, Z_DOWN.index(i), x + 1 - cx]
-                source = jnp.where(row_id == CZ - 1, jnp.broadcast_to(edge, (CZ, LANES)),
+                edge = zrecv[step, 1, Z_DOWN.index(i), x + 1 - cx, :, cut]
+                source = jnp.where(row_id == CZ - 1, jnp.broadcast_to(edge, (CZ, width)),
                                    pltpu.roll(source, CZ - 1, 0))
             if cy == 1:
                 source = pltpu.roll(source, 1, 1)
             elif cy == -1:
-                source = pltpu.roll(source, LANES - 1, 1)
-            write(i, jnp.where(masks[cy % 3] > 0.5, star[step, POS[OPPOSITE[i]], x + 1], source))
-
-    def write_temp(i, value):
-        temp[i] = value
-
-    def advance(x):
-        stream_plane(0, x, write_temp)
-        collide_planes(load_temp, store_star(1), x)
+                source = pltpu.roll(source, width - 1, 1)
+            bounced = star[step, POS[OPPOSITE[i]], x + 1, :, cut]
+            write(i, jnp.where(masks[cy % 3, :, cut] > 0.5, bounced, source))
+
+    def advance(x, cut=slice(0, LANES)):
+        def write(i, value):
+            temp[i, :, cut] = value
+        stream_plane(0, x, cut, write)
+        collide_planes(load_temp, store_star(1), x, range(cut.start // 128, cut.stop // 128))
 
     def finish(x):
         def write(i, value):
             pre_out[i, x] = value[:, 0:NP]
             main_out[i, x] = value[:, NP:]
-        stream_plane(1, x, write)
+        stream_plane(1, x, slice(0, LANES), write)
 
     def rows_start(step):
         @pl.when(st == 0)
@@ -192,7 +202,7 @@
         @pl.when(st == 0)
         def _():
             for d in range(1, ROWS):
-                row_copy(step, d).wait()
+                row_copy(step, d).wait_recv()
             for e in range(COLS):
                 target = row * COLS + lax.rem(col + e, COLS)
                 own = tile_ref[target]
@@ -211,7 +221,7 @@
         @pl.when(st == 0)
         def _():
             for e in range(1, COLS):
-                quad_copy(step, e).wait()
+                quad_copy(step, e).wait_recv()
             left_at = lax.rem(sp + SPAN - 1, SPAN)
             right_at = lax.rem(sp + 1, SPAN)
             tile = pay_recv[step][col_slot(tile_ref[sp]), 0:5]
@@ -219,8 +229,14 @@
                              pay_recv[step][col_slot(tile_ref[left_at]), 5],
                              pay_recv[step][col_slot(tile_ref[right_at]), 5])
             coarse = jnp.concatenate([tile.reshape(5 * CZ, 128), edge], axis=0)
-            fine = jnp.dot(coarse, spread[...], precision=lax.Precision.HIGHEST,
-                           preferred_element_type=jnp.float32)
+            high = coarse.astype(jnp.bfloat16)
+            rest = coarse - high.astype(jnp.float32)
+            middle = rest.astype(jnp.bfloat16)
+            low = (rest - middle.astype(jnp.float32)).astype(jnp.bfloat16)
+            parts = jnp.dot(jnp.concatenate([high, middle, low], axis=0), spread[...],
+                            preferred_element_type=jnp.float32)
+            count = 6 * CZ
+            fine = parts[0:count] + (parts[count:2 * count] + parts[2 * count:])
             own_phase = jnp.full((5 * CZ, NM), phase_ref[sp], jnp.int32)
             plane = jnp.where(own_phase == 0, fine[0:5 * CZ, 0:NM], fine[0:5 * CZ, NM:])
             plane = plane.reshape(5, CZ, NM)
@@ -242,7 +258,14 @@
             for way, pop in ((0, Z_UP.index(14)), (1, Z_DOWN.index(12))):
                 zrecv[step, way, pop, CX + 1, :, NP:] = zrecv[step, way, pop, CX, :, NP:]
 
-    collide_planes(load_input, store_star(0), CX - 1)
+    for load in loads:
+        load.wait()
+
+    def first(x, carry):
+        collide_planes(load_input, store_star(0), x)
+        return carry
+
+    lax.fori_loop(0, CX, first, 0)
 
     @pl.when(st == 0)
     def _():
@@ -252,20 +275,17 @@
     def _():
         pl.semaphore_wait(barrier, 8)
 
-    x_copy(0, 0).start()
+    def start(*copies):
+        for copy in copies:
+            copy.start()
+
+    def arrive(*copies):
+        for copy in copies:
+            copy.wait_recv()
+
     rows_start(0)
-    collide_planes(load_input, store_star(0), 0)
-    x_copy(0, 1).start()
-
-    def first(x, carry):
-        collide_planes(load_input, store_star(0), x)
-        return carry
-
-    lax.fori_loop(1, CX - 1, first, 0)
-    for way in range(2):
-        z_copy(0, way).start()
-    for which in range(4):
-        corner_copy(0, which).start()
+    start(corner_copy(0, 1), corner_copy(0, 2), x_copy(0, 1, 0), z_copy(0, 0), z_copy(0, 1),
+          x_copy(0, 0, 0), corner_copy(0, 0), corner_copy(0, 3), x_copy(0, 1, 1), x_copy(0, 0, 1))
 
     wall = jnp.broadcast_to(wall_ref[...].astype(jnp.float32), (CZ, NM))
     fine_id = lax.broadcasted_iota(jnp.int32, (NM, NP), 0)
@@ -292,68 +312,93 @@
             high = jnp.clip(lower + 1, 0, NP - 1)
             spread[:, phase * NM:(phase + 1) * NM] = (
                 jnp.where(coarse_row == low, 1.0 - upper, 0.0)
-                + jnp.where(coarse_row == high, upper, 0.0))
-
-    for step in range(2):
-        plane = advance if step == 0 else finish
-
+                + jnp.where(coarse_row == high, upper, 0.0)).astype(jnp.bfloat16)
+
+    def inside(plane):
         def inner(x, carry):
             plane(x)
             return carry
-
+        lax.fori_loop(1, CX - 1, inner, 0)
+
+    arrive(z_copy(0, 0), z_copy(0, 1), corner_copy(0, 1), corner_copy(0, 2), x_copy(0, 1, 0))
+    advance(CX - 1, PRE)
+    rows_start(1)
+    start(x_copy(1, 0, 0))
+    inside(advance)
+    arrive(x_copy(0, 1, 1))
+    outlet(0)
+    advance(CX - 1, MAIN)
+    start(x_copy(1, 0, 1), corner_copy(1, 0), corner_copy(1, 3))
+    quads_start(0)
+    arrive(x_copy(0, 0, 0), x_copy(0, 0, 1), corner_copy(0, 0), corner_copy(0, 3))
+    inlet(0)
+    advance(0)
+    start(z_copy(1, 0), z_copy(1, 1), corner_copy(1, 1), corner_copy(1, 2),
+          x_copy(1, 1, 0), x_copy(1, 1, 1))
+
+    quads_start(1)
+    arrive(z_copy(1, 0), z_copy(1, 1))
+    inside(finish)
+    arrive(corner_copy(1, 1), corner_copy(1, 2), x_copy(1, 1, 0), x_copy(1, 1, 1))
+    outlet(1)
+    finish(CX - 1)
+    arrive(x_copy(1, 0, 0), x_copy(1, 0, 1), corner_copy(1, 0), corner_copy(1, 3))
+    inlet(1)
+    finish(0)
+
+    for step in range(2):
         for way in range(2):
-            z_copy(step, way).wait()
-        lax.fori_loop(1, CX - 1, inner, 0)
-        quads_start(step)
-        for way in range(2):
-            x_copy(step, way).wait()
+            z_copy(step, way).wait_send()
+            for part in range(2):
+                x_copy(step, way, part).wait_send()
         for which in range(4):
-            corner_copy(step, which).wait()
-        outlet(step)
-        plane(CX - 1)
-        if step == 0:
-            x_copy(1, 0).start()
-            rows_start(1)
-        inlet(step)
-        plane(0)
-        if step == 0:
-            x_copy(1, 1).start()
-            for way in range(2):
-                z_copy(1, way).start()
-            for which in range(4):
-                corner_copy(1, which).start()
+            corner_copy(step, which).wait_send()
+
+    @pl.when(st == 0)
+    def _():
+        for step in range(2):
+            for d in range(1, ROWS):
+                row_copy(step, d).wait_send()
+            for e in range(1, COLS):
+                quad_copy(step, e).wait_send()
 
 
 def local(pre_pops, main_pops, tile_map, layer_phase, wall_flags):
     vmem = pl.BlockSpec(memory_space=pltpu.VMEM)
-    smem = pl.BlockSpec(memory_space=pltpu.SMEM)
+    hbm = pl.BlockSpec(memory_space=pltpu.HBM)
     dma = pltpu.SemaphoreType.DMA
     f32 = jnp.float32
     return pl.pallas_call(
         body,
         out_shape=(jax.ShapeDtypeStruct(pre_pops.shape, f32),
                    jax.ShapeDtypeStruct(main_pops.shape, f32)),
-        in_specs=[smem, smem, vmem, vmem, vmem],
+        in_specs=[hbm] * 5,
         out_specs=(vmem, vmem),
         scratch_shapes=[
+            pltpu.SMEM((SPAN,), jnp.int32),
+            pltpu.SMEM((SPAN,), jnp.int32),
+            pltpu.VMEM((1, NM), jnp.int32),
+            pltpu.VMEM((19, CX, CZ, NP), f32),
+            pltpu.VMEM((19, CX, CZ, NM), f32),
             pltpu.VMEM((2, 19, CX + 2, CZ, LANES), f32),
             pltpu.VMEM((2, 2, 5, CX, 1, LANES), f32),
             pltpu.VMEM((2, 2, 5, CX + 2, 1, LANES), f32),
             pltpu.VMEM((19, CZ, LANES), f32),
             pltpu.VMEM((3, CZ, LANES), f32),
-            pltpu.VMEM((NP, 2 * NM), f32),
+            pltpu.VMEM((NP, 2 * NM), jnp.bfloat16),
             pltpu.VMEM((ROWS, 5, CZ, NP), f32),
             pltpu.VMEM((ROWS, 5, CZ, NP), f32),
             pltpu.VMEM((2, COLS, 6, CZ, NP), f32),
             pltpu.VMEM((COLS, 6, CZ, NP), f32),
             pltpu.VMEM((COLS, 6, CZ, NP), f32),
-            dma((2, 2)), dma((2, 2)), dma((2, 2)), dma((2, 2)),
+            dma((2, 2, 2)), dma((2, 2, 2)), dma((2, 2)), dma((2, 2)),
             dma((2, 4)), dma((2, 4)),
-            dma((2, ROWS)), dma((2, ROWS)), dma((2, COLS)), dma((2, COLS)),
+            dma((2, ROWS)), dma((2, ROWS)), dma((2, COLS)), dma((2, COLS)), dma((5,)),
         ],
         compiler_params=pltpu.CompilerParams(
-            collective_id=0, has_side_effects=True, vmem_limit_bytes=60 * 1024 * 1024),
-    )(tile_map, layer_phase, wall_flags.reshape(1, NM), pre_pops, main_pops)
+            collective_id=0, has_side_effects=True, vmem_limit_bytes=20 * 1024 * 1024),
+    )(*[pltpu.with_memory_space_constraint(array, pltpu.HBM) for array in (
+        tile_map, layer_phase, wall_flags.reshape(1, NM), pre_pops, main_pops)])
 
 
 def solution(mesh):

time: 41.3 us -> 35.5 us (0.86)
  Pallas kernels: 37.3 us -> 32.9 us
  local copies, waits for them, and re-layouts: 3.1 us -> 1.86 us
    pallas_call x1, Pallas kernels: 37.3 us -> 32.9 us  [local(): pl.pallas_call(body, out_shape=(jax.ShapeDtypeStruct(pre_pops.shape, f32)...]
    unnamed x4 -> x2, local copies, waits for them, and re-layouts: 3.1 us -> 1.86 us
where the time goes in v1:
time: 35.5 us; the launch traced here: 35.4 us
  Pallas kernels  32.9 us (93%)
  local copies, waits for them, and re-layouts  1.86 us (5%)
  between operations  0.64 us (2%)
    pallas_call x1, Pallas kernels, local(): pl.pallas_call(body, out_shape=(jax.ShapeDtypeStruct(pre_pops.shape, f32)...  32.9 us
    unnamed x2, local copies, waits for them, and re-layouts  1.86 us

profile of v1, /device:TPU:1, one launch (start us, length us, event | category | flops | bytes accessed | tf_op | source)
XLA Modules:
  0.0 35.4 jit_solution(7598214071237884759)
XLA Ops:
  0.6 32.9 %shard_map.68 = (f32[19,8,8,128]{3,2,1,0:T(8,128)S(1)}, f32[19,8,8,256]{3,2,1,0:T(8,128)S(1)}) custom-call(s32[32]{0:T(128)} %tile_hbm.1, s32[32]{0:T(128)} %phase_hbm.1, s32[1,256]{1,0:T(1,128)} %bitcast.1, f32[19,8,8,128]{3,2,1,0:T(8,128)} %pre_hbm.1, f32[19,8,8,256]{3,2,1,0:T(8,128)} %main_hbm.1), custom_call_target="tpu_custom_call" | custom-call | tf_op jit(solution)/shard_map/pallas_call | solution.py:371
  33.5 0.8 %copy.9 = f32[19,8,8,128]{3,2,1,0:T(8,128)} copy(f32[19,8,8,128]{3,2,1,0:T(8,128)S(1)} %get-tuple-element.4) | data formatting | bytes 1245184
  34.4 1.0 %copy.10 = f32[19,8,8,256]{3,2,1,0:T(8,128)} copy(f32[19,8,8,256]{3,2,1,0:T(8,128)S(1)} %get-tuple-element.5) | data formatting | bytes 2490368

commit v2 on v1

--- a/solution.py
+++ b/solution.py
@@ -59,7 +59,7 @@
 
 def body(tile_hbm, phase_hbm, wall_hbm, pre_hbm, main_hbm, pre_out, main_out,
          tile_ref, phase_ref, wall_ref, pre_ref, main_ref, star, zsend, zrecv, temp, masks, spread, rows_a, rows_b, pay_send, pay_a, pay_b,
-         xs_sem, xr_sem, zs_sem, zr_sem, cs_sem, cr_sem, ys_sem, yr_sem, qs_sem, qr_sem, in_sem):
+         xs_sem, xr_sem, zs_sem, zr_sem, cs_sem, cr_sem, ys_sem, yr_sem, qs_sem, qr_sem, in_sem, ready_sem):
     rows_buf, pay_recv = (rows_a, rows_b), (pay_a, pay_b)
     st = lax.axis_index("stream")
     sp = lax.axis_index("span")
@@ -68,11 +68,13 @@
     row, col = lax.div(sp, COLS), lax.rem(sp, COLS)
 
     barrier = pltpu.get_barrier_semaphore()
-    for a in (st_up, st, st_down):
+    for a, b in ((st, sp_up), (st, sp_down), (st_down, sp_up), (st_down, sp), (st_down, sp_down)):
+        pl.semaphore_signal(barrier, inc=1, device_id=(a, b), device_id_type=MESH)
+
+    @pl.when(st != STREAM - 1)
+    def _():
         for b in (sp_up, sp, sp_down):
-            if a is st and b is sp:
-                continue
-            pl.semaphore_signal(barrier, inc=1, device_id=(a, b), device_id_type=MESH)
+            pl.semaphore_signal(barrier, inc=1, device_id=(st_up, b), device_id_type=MESH)
 
     @pl.when(st == 0)
     def _():
@@ -186,7 +188,7 @@
     def rows_start(step):
         @pl.when(st == 0)
         def _():
-            for d in range(1, ROWS):
+            for d in (4, 3, 5, 2, 6, 1, 7):
                 row_copy(step, d).start()
             rows_buf[step][0] = star[step, 0:5, CX, :, 0:NP]
 
@@ -269,11 +271,16 @@
 
     @pl.when(st == 0)
     def _():
-        pl.semaphore_wait(barrier, 8 + ROWS + COLS - 2)
+        pl.semaphore_wait(barrier, 5 + ROWS + COLS - 2)
 
     @pl.when(st != 0)
     def _():
         pl.semaphore_wait(barrier, 8)
+
+    @pl.when(st == STREAM - 1)
+    def _():
+        for b in (sp_up, sp, sp_down):
+            pl.semaphore_signal(ready_sem, inc=1, device_id=(st_up, b), device_id_type=MESH)
 
     def start(*copies):
         for copy in copies:
@@ -284,8 +291,18 @@
             copy.wait_recv()
 
     rows_start(0)
-    start(corner_copy(0, 1), corner_copy(0, 2), x_copy(0, 1, 0), z_copy(0, 0), z_copy(0, 1),
-          x_copy(0, 0, 0), corner_copy(0, 0), corner_copy(0, 3), x_copy(0, 1, 1), x_copy(0, 0, 1))
+
+    @pl.when(st != 0)
+    def _():
+        start(corner_copy(0, 1), corner_copy(0, 2), x_copy(0, 1, 0))
+
+    start(z_copy(0, 0), z_copy(0, 1), x_copy(0, 0, 0), corner_copy(0, 0), corner_copy(0, 3))
+
+    @pl.when(st != 0)
+    def _():
+        start(x_copy(0, 1, 1))
+
+    start(x_copy(0, 0, 1))
 
     wall = jnp.broadcast_to(wall_ref[...].astype(jnp.float32), (CZ, NM))
     fine_id = lax.broadcasted_iota(jnp.int32, (NM, NP), 0)
@@ -330,6 +347,12 @@
     advance(CX - 1, MAIN)
     start(x_copy(1, 0, 1), corner_copy(1, 0), corner_copy(1, 3))
     quads_start(0)
+
+    @pl.when(st == 0)
+    def _():
+        pl.semaphore_wait(ready_sem, 3)
+        start(corner_copy(0, 1), corner_copy(0, 2), x_copy(0, 1, 0), x_copy(0, 1, 1))
+
     arrive(x_copy(0, 0, 0), x_copy(0, 0, 1), corner_copy(0, 0), corner_copy(0, 3))
     inlet(0)
     advance(0)
@@ -393,7 +416,7 @@
             pltpu.VMEM((COLS, 6, CZ, NP), f32),
             dma((2, 2, 2)), dma((2, 2, 2)), dma((2, 2)), dma((2, 2)),
             dma((2, 4)), dma((2, 4)),
-            dma((2, ROWS)), dma((2, ROWS)), dma((2, COLS)), dma((2, COLS)), dma((5,)),
+            dma((2, ROWS)), dma((2, ROWS)), dma((2, COLS)), dma((2, COLS)), dma((5,)), pltpu.SemaphoreType.REGULAR,
         ],
         compiler_params=pltpu.CompilerParams(
             collective_id=0, has_side_effects=True, vmem_limit_bytes=20 * 1024 * 1024),

time: 35.5 us -> 32.2 us (0.907)
  Pallas kernels: 32.9 us -> 29.6 us
    pallas_call x1, Pallas kernels: 32.9 us -> 29.6 us  [local(): pl.pallas_call(body, out_shape=(jax.ShapeDtypeStruct(pre_pops.shape, f32)...]
where the time goes in v2:
time: 32.2 us; the launch traced here: 32.1 us
  Pallas kernels  29.6 us (92%)
  local copies, waits for them, and re-layouts  1.86 us (6%)
  between operations  0.64 us (2%)
    pallas_call x1, Pallas kernels, local(): pl.pallas_call(body, out_shape=(jax.ShapeDtypeStruct(pre_pops.shape, f32)...  29.6 us
    unnamed x2, local copies, waits for them, and re-layouts  1.86 us

profile of v2, /device:TPU:1, one launch (start us, length us, event | category | flops | bytes accessed | tf_op | source)
XLA Modules:
  0.0 32.1 jit_solution(16113509381918792059)
XLA Ops:
  0.6 29.6 %shard_map.68 = (f32[19,8,8,128]{3,2,1,0:T(8,128)S(1)}, f32[19,8,8,256]{3,2,1,0:T(8,128)S(1)}) custom-call(s32[32]{0:T(128)} %tile_hbm.1, s32[32]{0:T(128)} %phase_hbm.1, s32[1,256]{1,0:T(1,128)} %bitcast.1, f32[19,8,8,128]{3,2,1,0:T(8,128)} %pre_hbm.1, f32[19,8,8,256]{3,2,1,0:T(8,128)} %main_hbm.1), custom_call_target="tpu_custom_call" | custom-call | tf_op jit(solution)/shard_map/pallas_call | solution.py:394
  30.2 0.8 %copy.9 = f32[19,8,8,128]{3,2,1,0:T(8,128)} copy(f32[19,8,8,128]{3,2,1,0:T(8,128)S(1)} %get-tuple-element.4) | data formatting | bytes 1245184
  31.1 1.0 %copy.10 = f32[19,8,8,256]{3,2,1,0:T(8,128)} copy(f32[19,8,8,256]{3,2,1,0:T(8,128)S(1)} %get-tuple-element.5) | data formatting | bytes 2490368

commit v3 on v2

--- a/solution.py
+++ b/solution.py
@@ -282,6 +282,23 @@
         for b in (sp_up, sp, sp_down):
             pl.semaphore_signal(ready_sem, inc=1, device_id=(st_up, b), device_id_type=MESH)
 
+    last = STREAM - 1
+
+    def main_start(step, way):
+        @pl.when(st != (last if way == 0 else 0))
+        def _():
+            x_copy(step, way, 1).start()
+
+    def main_arrive(step, way):
+        @pl.when(st != (0 if way == 0 else last))
+        def _():
+            x_copy(step, way, 1).wait_recv()
+
+    def main_sent(step, way):
+        @pl.when(st != (last if way == 0 else 0))
+        def _():
+            x_copy(step, way, 1).wait_send()
+
     def start(*copies):
         for copy in copies:
             copy.start()
@@ -298,11 +315,8 @@
 
     start(z_copy(0, 0), z_copy(0, 1), x_copy(0, 0, 0), corner_copy(0, 0), corner_copy(0, 3))
 
-    @pl.when(st != 0)
-    def _():
-        start(x_copy(0, 1, 1))
-
-    start(x_copy(0, 0, 1))
+    main_start(0, 1)
+    main_start(0, 0)
 
     wall = jnp.broadcast_to(wall_ref[...].astype(jnp.float32), (CZ, NM))
     fine_id = lax.broadcasted_iota(jnp.int32, (NM, NP), 0)
@@ -337,43 +351,59 @@
             return carry
         lax.fori_loop(1, CX - 1, inner, 0)
 
-    arrive(z_copy(0, 0), z_copy(0, 1), corner_copy(0, 1), corner_copy(0, 2), x_copy(0, 1, 0))
-    advance(CX - 1, PRE)
-    rows_start(1)
-    start(x_copy(1, 0, 0))
-    inside(advance)
-    arrive(x_copy(0, 1, 1))
-    outlet(0)
-    advance(CX - 1, MAIN)
-    start(x_copy(1, 0, 1), corner_copy(1, 0), corner_copy(1, 3))
-    quads_start(0)
-
     @pl.when(st == 0)
     def _():
+        arrive(z_copy(0, 0), z_copy(0, 1), corner_copy(0, 1), corner_copy(0, 2), x_copy(0, 1, 0))
+        advance(CX - 1, PRE)
+        rows_start(1)
+        start(x_copy(1, 0, 0))
+        inside(advance)
+        main_arrive(0, 1)
+        advance(CX - 1, MAIN)
+        main_start(1, 0)
+        start(corner_copy(1, 0), corner_copy(1, 3))
+        quads_start(0)
         pl.semaphore_wait(ready_sem, 3)
-        start(corner_copy(0, 1), corner_copy(0, 2), x_copy(0, 1, 0), x_copy(0, 1, 1))
-
-    arrive(x_copy(0, 0, 0), x_copy(0, 0, 1), corner_copy(0, 0), corner_copy(0, 3))
-    inlet(0)
-    advance(0)
-    start(z_copy(1, 0), z_copy(1, 1), corner_copy(1, 1), corner_copy(1, 2),
-          x_copy(1, 1, 0), x_copy(1, 1, 1))
-
-    quads_start(1)
+        start(corner_copy(0, 1), corner_copy(0, 2), x_copy(0, 1, 0))
+        arrive(x_copy(0, 0, 0), corner_copy(0, 0), corner_copy(0, 3))
+        inlet(0)
+        advance(0)
+        start(z_copy(1, 0), z_copy(1, 1), corner_copy(1, 1), corner_copy(1, 2), x_copy(1, 1, 0))
+        quads_start(1)
+
+    @pl.when(st != 0)
+    def _():
+        arrive(z_copy(0, 0), z_copy(0, 1))
+        inside(advance)
+        arrive(x_copy(0, 0, 0), corner_copy(0, 0), corner_copy(0, 3))
+        main_arrive(0, 0)
+        advance(0)
+        start(x_copy(1, 1, 0), corner_copy(1, 1), corner_copy(1, 2))
+        main_start(1, 1)
+        arrive(x_copy(0, 1, 0), corner_copy(0, 1), corner_copy(0, 2))
+        main_arrive(0, 1)
+        outlet(0)
+        advance(CX - 1)
+        start(x_copy(1, 0, 0), corner_copy(1, 0), corner_copy(1, 3))
+        main_start(1, 0)
+        start(z_copy(1, 0), z_copy(1, 1))
+
     arrive(z_copy(1, 0), z_copy(1, 1))
     inside(finish)
-    arrive(corner_copy(1, 1), corner_copy(1, 2), x_copy(1, 1, 0), x_copy(1, 1, 1))
+    arrive(corner_copy(1, 1), corner_copy(1, 2), x_copy(1, 1, 0))
+    main_arrive(1, 1)
     outlet(1)
     finish(CX - 1)
-    arrive(x_copy(1, 0, 0), x_copy(1, 0, 1), corner_copy(1, 0), corner_copy(1, 3))
+    arrive(x_copy(1, 0, 0), corner_copy(1, 0), corner_copy(1, 3))
+    main_arrive(1, 0)
     inlet(1)
     finish(0)
 
     for step in range(2):
         for way in range(2):
             z_copy(step, way).wait_send()
-            for part in range(2):
-                x_copy(step, way, part).wait_send()
+            x_copy(step, way, 0).wait_send()
+            main_sent(step, way)
         for which in range(4):
             corner_copy(step, which).wait_send()
 
@@ -386,12 +416,21 @@
                 quad_copy(step, e).wait_send()
 
 
+def put(pre_in, main_in, pre_out, main_out, sem):
+    copies = [pltpu.make_async_copy(pre_in, pre_out, sem.at[0]),
+              pltpu.make_async_copy(main_in, main_out, sem.at[1])]
+    for copy in copies:
+        copy.start()
+    for copy in copies:
+        copy.wait()
+
+
 def local(pre_pops, main_pops, tile_map, layer_phase, wall_flags):
     vmem = pl.BlockSpec(memory_space=pltpu.VMEM)
     hbm = pl.BlockSpec(memory_space=pltpu.HBM)
     dma = pltpu.SemaphoreType.DMA
     f32 = jnp.float32
-    return pl.pallas_call(
+    outs = pl.pallas_call(
         body,
         out_shape=(jax.ShapeDtypeStruct(pre_pops.shape, f32),
                    jax.ShapeDtypeStruct(main_pops.shape, f32)),
@@ -422,6 +461,15 @@
             collective_id=0, has_side_effects=True, vmem_limit_bytes=20 * 1024 * 1024),
     )(*[pltpu.with_memory_space_constraint(array, pltpu.HBM) for array in (
         tile_map, layer_phase, wall_flags.reshape(1, NM), pre_pops, main_pops)])
+    return pl.pallas_call(
+        put,
+        out_shape=(jax.ShapeDtypeStruct(pre_pops.shape, f32),
+                   jax.ShapeDtypeStruct(main_pops.shape, f32)),
+        in_specs=[vmem] * 2,
+        out_specs=(hbm, hbm),
+        scratch_shapes=[dma((2,))],
+        compiler_params=pltpu.CompilerParams(vmem_limit_bytes=1024 * 1024),
+    )(*outs)
 
 
 def solution(mesh):

time: 32.2 us -> 30.4 us (0.944)
  local copies, waits for them, and re-layouts: 1.86 us -> 0 us
    unnamed x2 -> x0, local copies, waits for them, and re-layouts: 1.86 us -> none
    pallas_call x0 -> x1, Pallas kernels: none -> 1.26 us  [local(): pl.pallas_call(put, out_shape=(jax.ShapeDtypeStruct(pre_pops.shape, f32),...]
    pallas_call x1, Pallas kernels: 29.6 us -> 28.4 us  [local(): pl.pallas_call(body, out_shape=(jax.ShapeDtypeStruct(pre_pops.shape, f32)...]
where the time goes in v3:
time: 30.4 us; the launch traced here: 30.3 us
  Pallas kernels  29.6 us (97%)
  between operations  0.64 us (2%)
    pallas_call x1, Pallas kernels, local(): pl.pallas_call(body, out_shape=(jax.ShapeDtypeStruct(pre_pops.shape, f32)...  28.4 us
    pallas_call x1, Pallas kernels, local(): pl.pallas_call(put, out_shape=(jax.ShapeDtypeStruct(pre_pops.shape, f32),...  1.26 us

profile of v3, /device:TPU:1, one launch (start us, length us, event | category | flops | bytes accessed | tf_op | source)
XLA Modules:
  0.0 30.3 jit_solution(8554197120129388096)
XLA Ops:
  0.6 28.4 %shard_map.68 = (f32[19,8,8,128]{3,2,1,0:T(8,128)S(1)}, f32[19,8,8,256]{3,2,1,0:T(8,128)S(1)}) custom-call(s32[32]{0:T(128)} %tile_hbm.1, s32[32]{0:T(128)} %phase_hbm.1, s32[1,256]{1,0:T(1,128)} %bitcast.1, f32[19,8,8,128]{3,2,1,0:T(8,128)} %pre_hbm.1, f32[19,8,8,256]{3,2,1,0:T(8,128)} %main_hbm.1), custom_call_target="tpu_custom_call" | custom-call | tf_op jit(solution)/shard_map/pallas_call | solution.py:433
  29.0 1.3 %shard_map.69 = (f32[19,8,8,128]{3,2,1,0:T(8,128)}, f32[19,8,8,256]{3,2,1,0:T(8,128)}) custom-call(f32[19,8,8,128]{3,2,1,0:T(8,128)S(1)} %get-tuple-element.4.pre_in, f32[19,8,8,256]{3,2,1,0:T(8,128)S(1)} %get-tuple-element.5.main_in), custom_call_target="tpu_custom_call" | custom-call | tf_op jit(solution)/shard_map/pallas_call | solution.py:464

commit v4 on v3

--- a/solution.py
+++ b/solution.py
@@ -71,7 +71,7 @@
     for a, b in ((st, sp_up), (st, sp_down), (st_down, sp_up), (st_down, sp), (st_down, sp_down)):
         pl.semaphore_signal(barrier, inc=1, device_id=(a, b), device_id_type=MESH)
 
-    @pl.when(st != STREAM - 1)
+    @pl.when(st < STREAM - 2)
     def _():
         for b in (sp_up, sp, sp_down):
             pl.semaphore_signal(barrier, inc=1, device_id=(st_up, b), device_id_type=MESH)
@@ -273,11 +273,15 @@
     def _():
         pl.semaphore_wait(barrier, 5 + ROWS + COLS - 2)
 
-    @pl.when(st != 0)
+    @pl.when((st > 0) & (st < STREAM - 1))
     def _():
         pl.semaphore_wait(barrier, 8)
 
     @pl.when(st == STREAM - 1)
+    def _():
+        pl.semaphore_wait(barrier, 5)
+
+    @pl.when(st >= STREAM - 2)
     def _():
         for b in (sp_up, sp, sp_down):
             pl.semaphore_signal(ready_sem, inc=1, device_id=(st_up, b), device_id_type=MESH)
@@ -309,13 +313,16 @@
 
     rows_start(0)
 
-    @pl.when(st != 0)
+    @pl.when((st > 0) & (st < last))
     def _():
         start(corner_copy(0, 1), corner_copy(0, 2), x_copy(0, 1, 0))
 
     start(z_copy(0, 0), z_copy(0, 1), x_copy(0, 0, 0), corner_copy(0, 0), corner_copy(0, 3))
 
-    main_start(0, 1)
+    @pl.when((st > 0) & (st < last))
+    def _():
+        x_copy(0, 1, 1).start()
+
     main_start(0, 0)
 
     wall = jnp.broadcast_to(wall_ref[...].astype(jnp.float32), (CZ, NM))
@@ -358,13 +365,13 @@
         rows_start(1)
         start(x_copy(1, 0, 0))
         inside(advance)
+        pl.semaphore_wait(ready_sem, 3)
+        start(corner_copy(0, 1), corner_copy(0, 2), x_copy(0, 1, 0))
         main_arrive(0, 1)
         advance(CX - 1, MAIN)
         main_start(1, 0)
         start(corner_copy(1, 0), corner_copy(1, 3))
         quads_start(0)
-        pl.semaphore_wait(ready_sem, 3)
-        start(corner_copy(0, 1), corner_copy(0, 2), x_copy(0, 1, 0))
         arrive(x_copy(0, 0, 0), corner_copy(0, 0), corner_copy(0, 3))
         inlet(0)
         advance(0)
@@ -375,17 +382,23 @@
     def _():
         arrive(z_copy(0, 0), z_copy(0, 1))
         inside(advance)
-        arrive(x_copy(0, 0, 0), corner_copy(0, 0), corner_copy(0, 3))
-        main_arrive(0, 0)
-        advance(0)
-        start(x_copy(1, 1, 0), corner_copy(1, 1), corner_copy(1, 2))
-        main_start(1, 1)
+
+        @pl.when(st == last)
+        def _():
+            pl.semaphore_wait(ready_sem, 3)
+            start(corner_copy(0, 1), corner_copy(0, 2), x_copy(0, 1, 0), x_copy(0, 1, 1))
+
         arrive(x_copy(0, 1, 0), corner_copy(0, 1), corner_copy(0, 2))
         main_arrive(0, 1)
         outlet(0)
         advance(CX - 1)
         start(x_copy(1, 0, 0), corner_copy(1, 0), corner_copy(1, 3))
         main_start(1, 0)
+        arrive(x_copy(0, 0, 0), corner_copy(0, 0), corner_copy(0, 3))
+        main_arrive(0, 0)
+        advance(0)
+        start(x_copy(1, 1, 0), corner_copy(1, 1), corner_copy(1, 2))
+        main_start(1, 1)
         start(z_copy(1, 0), z_copy(1, 1))
 
     arrive(z_copy(1, 0), z_copy(1, 1))

time: 30.4 us -> 30.3 us (level)
  no operation moved by 1% of the time
where the time goes in v4:
time: 30.3 us; the launch traced here: 30.2 us
  Pallas kernels  29.5 us (97%)
  between operations  0.64 us (2%)
    pallas_call x1, Pallas kernels, local(): pl.pallas_call(body, out_shape=(jax.ShapeDtypeStruct(pre_pops.shape, f32)...  28.3 us
    pallas_call x1, Pallas kernels, local(): pl.pallas_call(put, out_shape=(jax.ShapeDtypeStruct(pre_pops.shape, f32),...  1.26 us

profile of v4, /device:TPU:1, one launch (start us, length us, event | category | flops | bytes accessed | tf_op | source)
XLA Modules:
  0.0 30.2 jit_solution(18222380645209099872)
XLA Ops:
  0.6 28.3 %shard_map.68 = (f32[19,8,8,128]{3,2,1,0:T(8,128)S(1)}, f32[19,8,8,256]{3,2,1,0:T(8,128)S(1)}) custom-call(s32[32]{0:T(128)} %tile_hbm.1, s32[32]{0:T(128)} %phase_hbm.1, s32[1,256]{1,0:T(1,128)} %bitcast.1, f32[19,8,8,128]{3,2,1,0:T(8,128)} %pre_hbm.1, f32[19,8,8,256]{3,2,1,0:T(8,128)} %main_hbm.1), custom_call_target="tpu_custom_call" | custom-call | tf_op jit(solution)/shard_map/pallas_call | solution.py:446
  28.9 1.3 %shard_map.69 = (f32[19,8,8,128]{3,2,1,0:T(8,128)}, f32[19,8,8,256]{3,2,1,0:T(8,128)}) custom-call(f32[19,8,8,128]{3,2,1,0:T(8,128)S(1)} %get-tuple-element.4.pre_in, f32[19,8,8,256]{3,2,1,0:T(8,128)S(1)} %get-tuple-element.5.main_in), custom_call_target="tpu_custom_call" | custom-call | tf_op jit(solution)/shard_map/pallas_call | solution.py:477
